TPU v7x, 256 devices: a whole 4x4x8 slice. The times are simulated.
256 devices in a mesh: sec: 2 (over y_hi), col: 8 (over z), row: 16 (over y_lo, x, core).
Axes of the slice: x: 4, y: 4 (y_hi: 2, y_lo: 2; y = y_hi * 2 + y_lo), z: 8, core: 2. Of those that a mesh axis runs over, the one named last changes fastest.
Arguments:
- ancestor: float32 [16384, 16384], P('row', ('sec', 'col')), may hold values from -0.3 to 0.3
- panel: float32 [2, 8192, 2048], P('sec', 'row', 'col'), may hold values from -1.5 to 1.5
- diag_inverse: float32 [2, 2048, 2048], P('sec', 'col', 'row'), may hold values from -12 to 12
- frontier: int32 [2, 16, 4], replicated, may hold values from 0 to 7, as said below
- counts: int32 [2, 16], replicated, may hold values from 1 to 4
- pattern: int32 [2, 64, 64], replicated, may hold values 0 or 1
Outputs:
- cross_block: float32 [2, 2048, 8192], P('sec', 'col', 'row')
- inverse: float32 [2, 2048, 2048], P('sec', 'col', 'row')
Inputs may be any that keep to these rules, and one draw needn't show every extreme that they name: The 4 offsets of one child and group are distinct; slot j of group g is ancestor tile 8 * g + frontier[c, g, j]. Slots j >= counts[c, g] of group g are padding for child c.
All inputs are finite; a program needn't handle non-finite values.
Results may differ from a plain program's by a relative error of at most 0.0001.
Values sent between devices are 32-bit elements; how exact they have to be, the bound alone decides.
No kernel may reach another device: no remote copies, remote signals or barrier semaphores. Data moves between devices by JAX's collectives and lax.ppermute only.
A program may use at most 128 MiB of HBM per device.

v0:
```python
import functools

import jax
import jax.numpy as jnp
from jax import lax
from jax.experimental import pallas as pl
from jax.experimental.pallas import tpu as pltpu
from jax.sharding import PartitionSpec as P


TILE = 128
SLOTS = 4


Z, Y, X, CORES = 8, 2, 4, 2


def row_of(y, x, c):
    return (y % Y) * X * CORES + (x % X) * CORES + c


def row_pairs(move):
    places = [(y, x, c) for y in range(Y) for x in range(X) for c in range(CORES)]
    return [(row_of(*place), row_of(*move(*place))) for place in places]


def along_x(value, step):
    return lax.ppermute(value, "row", row_pairs(lambda y, x, c: (y, x + step, c)))


def across_y(value):
    return lax.ppermute(value, "row", row_pairs(lambda y, x, c: (y + 1, x, c)))


def across_core(value):
    return lax.ppermute(value, "row", row_pairs(lambda y, x, c: (y, x, 1 - c)))


def across_sec(value):
    return lax.ppermute(value, "sec", [(0, 1), (1, 0)])


def along_z(value, step):
    return lax.ppermute(value, "col", [(z, (z + step) % Z) for z in range(Z)])


def dot(left, right, dims):
    return lax.dot_general(
        left,
        right,
        (dims, ((), ())),
        precision=lax.Precision.HIGH,
        preferred_element_type=jnp.float32,
    )


def pick_kernel(place, ancestor, out, sems):
    tiles = [(a, b) for a in range(SLOTS) for b in range(SLOTS)]

    def spot(a, b):
        return (pl.ds(a * TILE, TILE), pl.ds(b * TILE, TILE))

    copies = []
    for a, b in tiles:
        first = pl.multiple_of(place[0, a] * TILE, TILE)
        second = pl.multiple_of(place[1, b] * TILE, TILE)
        source = ancestor.at[pl.ds(first, TILE), pl.ds(second, TILE)]
        copies.append(pltpu.make_async_copy(source, out.at[spot(a, b)], sems.at[a, b]))
        copies[-1].start()
    for (a, b), copy in zip(tiles, copies):
        copy.wait()
        out[spot(a, b)] = out[spot(a, b)] * place[2 + a, b].astype(jnp.float32)


def places(frontier, counts, pattern, block, group):
    ids = jnp.arange(SLOTS, dtype=jnp.int32)

    def at(table, index):
        return lax.dynamic_index_in_dim(table, index, 1, keepdims=False)

    row_live = ids[None, :] < at(counts, group)[:, None]
    column_live = ids[None, :] < at(counts, block)[:, None]
    start = (jnp.int32(0), group * SLOTS, block * SLOTS)
    near = lax.dynamic_slice(pattern, start, (2, SLOTS, SLOTS))
    mask = jnp.where(row_live[:, :, None] & column_live[:, None, :], near, 0)
    return jnp.concatenate([at(frontier, group)[:, None], at(frontier, block)[:, None], mask], axis=1)


def pick_tiles(ancestor, place):
    edge = SLOTS * TILE
    return pl.pallas_call(
        pick_kernel,
        grid_spec=pltpu.PrefetchScalarGridSpec(
            num_scalar_prefetch=1,
            grid=(),
            in_specs=[pl.BlockSpec(memory_space=pl.ANY)],
            out_specs=pl.BlockSpec(memory_space=pltpu.VMEM),
            scratch_shapes=[pltpu.SemaphoreType.DMA((SLOTS, SLOTS))],
        ),
        out_shape=jax.ShapeDtypeStruct((edge, edge), jnp.float32),
        cost_estimate=pl.CostEstimate(
            flops=edge * edge, bytes_accessed=8 * edge * edge, transcendentals=0
        ),
        name="pick_tiles",
    )(place, ancestor)


def two_terms(value):
    high = value.astype(jnp.bfloat16)
    return high, (value - high.astype(jnp.float32)).astype(jnp.bfloat16)


def split_kernel(mine, partner, sibling_mine, sibling_partner, high, low):
    edge = SLOTS * TILE
    for i, row in enumerate(((mine, partner), (sibling_mine, sibling_partner))):
        for j, ref in enumerate(row):
            spot = (pl.ds(i * edge, edge), pl.ds(j * edge, edge))
            high[spot], low[spot] = two_terms(ref[...])


def split_tiles(*tiles):
    edge = SLOTS * TILE
    shape = jax.ShapeDtypeStruct((2 * edge, 2 * edge), jnp.bfloat16)
    return pl.pallas_call(
        split_kernel,
        out_shape=(shape, shape),
        cost_estimate=pl.CostEstimate(flops=12 * edge * edge, bytes_accessed=32 * edge * edge, transcendentals=0),
        name="split_tiles",
    )(*tiles)


STEP = 512


def partial_kernel(spots, whole, where, *refs):
    count = len(spots)
    taken = count + (not whole)
    blocks, (high, low) = refs[:taken], refs[taken : taken + 2]
    parts, block_high, block_low, total, sems = refs[-5:]
    edge = SLOTS * TILE
    k = pl.program_id(0)
    y, x, z, c, flip = (where[i] for i in range(5))

    @pl.when(k == 0)
    def _():
        for j in range(count):
            for half in range(2):
                if whole or j < count - 1:
                    start = pl.multiple_of((half ^ flip) * edge, edge)
                    value = blocks[j][pl.ds(start, edge), :]
                else:
                    value = jnp.where(flip == 0, blocks[j + half][...], blocks[j + 1 - half][...])
                spot = (pl.ds(j * TILE, TILE), pl.ds(half * edge, edge))
                block_high[spot], block_low[spot] = two_terms(value.T)

    def product(left, right):
        return lax.dot_general(
            left[...], right[...], (((1,), (1,)), ((), ())), preferred_element_type=jnp.float32
        )

    total[k] = product(block_high, high) + product(block_low, high) + product(block_high, low)

    def copies(step):
        columns = pl.ds(pl.multiple_of(step * STEP, STEP), STEP)
        found = []
        for j, (dy, dx) in enumerate(spots):
            chip = lax.rem(y + dy, Y) * X + lax.rem(x + dx, X)
            distance = lax.rem(chip + 16 - 2 * z + 4 * c, Z)
            source = total.at[step, pl.ds(j * TILE, TILE), :]
            target = parts.at[distance, :, columns]
            found.append(pltpu.make_async_copy(source, target, sems.at[step, j]))
        return found

    for copy in copies(k):
        copy.start()

    @pl.when(k == pl.num_programs(0) - 1)
    def _():
        @pl.loop(0, 2 * edge // STEP)
        def _(step):
            for copy in copies(step):
                copy.wait()


def partial_products(spots, blocks, where, high, low, parts=None):
    count = len(spots)
    edge = SLOTS * TILE
    steps = 2 * edge // STEP
    vmem = pl.BlockSpec(memory_space=pltpu.VMEM)
    anywhere = pl.BlockSpec(memory_space=pl.ANY)
    tile_rows = pl.BlockSpec((STEP, 2 * edge), lambda k, where: (k, 0))
    args = [where, *blocks, high, low]
    if parts is not None:
        args.append(parts)
    rows = count * TILE
    return pl.pallas_call(
        functools.partial(partial_kernel, spots, len(blocks) == count),
        grid_spec=pltpu.PrefetchScalarGridSpec(
            num_scalar_prefetch=1,
            grid=(steps,),
            in_specs=[vmem] * len(blocks) + [tile_rows] * 2 + [anywhere] * (parts is not None),
            out_specs=anywhere,
            scratch_shapes=[
                pltpu.VMEM((rows, 2 * edge), jnp.bfloat16),
                pltpu.VMEM((rows, 2 * edge), jnp.bfloat16),
                pltpu.VMEM((steps, rows, STEP), jnp.float32),
                pltpu.SemaphoreType.DMA((steps, count)),
            ],
        ),
        out_shape=jax.ShapeDtypeStruct((Z, TILE, 2 * edge), jnp.float32),
        input_output_aliases={} if parts is None else {len(args) - 1: 0},
        cost_estimate=pl.CostEstimate(
            flops=6 * rows * 4 * edge * edge,
            bytes_accessed=4 * edge * (4 * edge + 4 * rows),
            transcendentals=0,
        ),
        name="partial_products",
    )(*args)


def to_chips(panel):
    low, high = panel[:, :TILE], panel[:, TILE:]
    y = lax.axis_index("row") // (X * CORES)
    first = jnp.where(y == 0, low, high)
    second = jnp.where(y == 0, high, low)

    def pairs(flip):
        found = []
        for z in range(Z):
            for g in range(16):
                c = (g // Z) ^ flip
                chip = (z + g % Z + 4 * c) % Z
                found.append((z * 16 + g, z * 16 + chip * CORES + c))
        return found

    first = lax.ppermute(first, ("col", "row"), pairs(0))
    second = lax.ppermute(second, ("col", "row"), pairs(1))
    return first, second


def mirrored(value):
    pairs = []
    for z in range(Z):
        for chip in range(8):
            for c in range(CORES):
                place = chip * CORES + c
                pairs.append((z * 16 + place, (chip - z + 4 * c) % Z * 16 + place))
    return lax.ppermute(value, ("col", "row"), pairs)


def scattered_along_z(parts):
    half = parts.shape[1] // 2

    def term(distance, which):
        return parts[distance % Z, which * half : (which + 1) * half]

    up_a, down_b = along_z(term(4, 0), 1), along_z(term(4, 1), -1)
    up_b, down_a = along_z(term(3, 1), 1), along_z(term(-3, 0), -1)
    for distance in (3, 2, 1):
        sums = up_a + term(distance, 0), down_b + term(-distance, 1)
        up_a, down_b = along_z(sums[0], 1), along_z(sums[1], -1)
        if distance > 1:
            up_b, down_a, *_ = together(up_b, down_a, *sums)
            sums = up_b + term(distance - 1, 1), down_a + term(1 - distance, 0)
            up_b, down_a = along_z(sums[0], 1), along_z(sums[1], -1)
            up_a, down_b, *_ = together(up_a, down_b, *sums)
    return jnp.concatenate([term(0, 0) + up_a + down_a, term(0, 1) + up_b + down_b], axis=0)


def scattered_in_plane(terms):
    groups = []
    for z in range(Z):
        for c in range(CORES):
            groups.append([z * 16 + (z + d) % Z * CORES + c for d in range(Z)])
    arrived = lax.all_to_all(terms, ("col", "row"), 0, 0, axis_index_groups=groups, tiled=True)
    return jnp.sum(arrived, axis=0)


def together(*values):
    return lax.optimization_barrier(values)


def per_device(ancestor, panel, diag_inverse, frontier, counts, pattern):
    s = lax.axis_index("sec")
    z = lax.axis_index("col")
    row = lax.axis_index("row")
    y, x, c = row // 8, row // 2 % 4, row % 2
    edge = SLOTS * TILE

    both_places = places(frontier, counts, pattern, s * Z + z, row)

    def pick(child):
        place = lax.dynamic_index_in_dim(both_places, child, 0, keepdims=False)
        return pick_tiles(ancestor, place)

    low, high = panel[0][:, :TILE], panel[0][:, TILE:]
    first, second = to_chips(panel[0])
    sibling_rows = across_core(jnp.where(c == 0, high, low))
    own_rows = jnp.concatenate([jnp.where(c == 0, low, high), sibling_rows], axis=0)
    up1 = along_z(own_rows, 1)
    down1 = along_z(own_rows, -1)
    theirs = pick(1 - s)
    partner = across_sec(theirs)
    own_columns = mirrored(jnp.concatenate([first, second], axis=0))
    mine = pick(s)
    sibling_mine = across_core(mine)
    sibling_partner = across_core(partner)
    tiles_high, tiles_low = split_tiles(mine, partner, sibling_mine, sibling_partner)

    where = jnp.stack([y, x, z, c, s ^ c]).astype(jnp.int32)

    def placed(spots, blocks, parts=None):
        return partial_products(spots, blocks, where, tiles_high, tiles_low, parts)

    left = along_x(own_columns, 1)
    right = along_x(own_columns, -1)
    over = across_y(own_columns)
    up2 = along_z(up1, 1)
    down2 = along_z(down1, -1)
    far = along_x(left, 1)
    over_right = along_x(over, -1)
    over_left = across_y(left)
    up3 = along_z(up2, 1)
    down3 = along_z(down2, -1)
    half = SLOTS * TILE
    spots = ((0, 3), (0, 1), (1, 0), (0, 0))
    parts = placed(spots, [left, right, over, own_columns])
    far_a = along_x(over_left[:half], 1)
    far_b = along_x(over_right[half:], -1)
    up4 = along_z(up3[:half], 1)
    down4 = along_z(down3[half:], -1)
    z_far = jnp.concatenate([up4, down4], axis=0)
    spots = ((0, 2), (1, 1), (1, 3), (1, 2))
    parts = placed(spots, [far, over_right, over_left, far_a, far_b], parts)
    rows_full = jnp.stack([own_rows, down1, down2, down3, z_far, up3, up2, up1])
    reduced = scattered_along_z(parts)

    received = across_core(reduced)
    received = jnp.concatenate([received[:, edge:], received[:, :edge]], axis=1)
    halves = [dot(rows_full, half, ((1,), (1,))) for half in (reduced, received)]
    halves = [jnp.transpose(half, (0, 2, 1)) for half in halves]

    def ordered(value, other):
        return jnp.where(
            c == 0,
            jnp.concatenate([value, other], axis=0),
            jnp.concatenate([other, value], axis=0),
        )

    summed = scattered_in_plane(jnp.concatenate(halves, axis=1))
    cross_part = -ordered(reduced[:, :edge], received[:, :edge])
    inverse_part = diag_inverse[0] + ordered(summed[:TILE], summed[TILE:])
    return (cross_part[None], inverse_part[None])


def solution(mesh):
    return jax.shard_map(
        per_device,
        mesh=mesh,
        in_specs=(
            P("row", ("sec", "col")),
            P("sec", "row", "col"),
            P("sec", "col", "row"),
            P(),
            P(),
            P(),
        ),
        out_specs=(P("sec", "col", "row"), P("sec", "col", "row")),
        check_vma=False,
    )
```

profile of v0, /device:TPU:3, one launch (start us, length us, event | category | flops | bytes accessed | tf_op | source)
XLA Modules:
  0.0 195.1 jit_solution(1928552448574295408)
XLA Ops:
  1.8 4.8 %collective-permute-start.1 = (f32[512,128]{1,0:T(8,128)S(1)}, f32[512,128]{1,0:T(8,128)S(1)}, u32[]{:S(2)}, u32[]{:S(2)}) collective-permute-start(f32[512,128]{1,0:T(8,128)S(1)} %get-tuple-element.44), channel_id=1, source_target_pairs={{0,9},{1,11},{2,13},{3,15},{4,1},{5,3},{6,5},{7,7},{8,0},{9,2},{10... | collective-permute-start | bytes 786440 | tf_op jit(solution)/shard_map/ppermute | solution.py:237
  12.0 3.1 %pick_tiles.3 = f32[512,512]{1,0:T(8,128)} custom-call(s32[6,4]{1,0:T(8,128)} %get-tuple-element.47.place, f32[1024,1024]{1,0:T(8,128)} %ancestor.3), custom_call_target="tpu_custom_call" | custom-call | flops 262144 | bytes 2097152 | tf_op jit(solution)/shard_map/pick_tiles/pallas_call | solution.py:91
  15.1 2.8 %collective-permute-start.10 = (f32[512,512]{1,0:T(8,128)}, f32[512,512]{1,0:T(8,128)S(1)}, u32[]{:S(2)}, u32[]{:S(2)}) collective-permute-start(f32[512,512]{1,0:T(8,128)} %pick_tiles.3), channel_id=1, source_target_pairs={{0,128},{128,0},{1,129},{129,1},{2,130},{130,2},{3,131},{131,3},{4... | collective-permute-start | bytes 3145736 | tf_op jit(solution)/shard_map/ppermute | solution.py:40
  17.9 9.0 %collective-permute-start.2 = (f32[1024,128]{1,0:T(8,128)S(1)}, f32[1024,128]{1,0:T(8,128)S(1)}, u32[]{:S(2)}, u32[]{:S(2)}) collective-permute-start(f32[1024,128]{1,0:T(8,128)S(1)} %pad_maximum_fusion.2), channel_id=1, source_target_pairs={{0,0},{1,65},{2,18},{3,83},{4,36},{5,101},{6,54},{7,119},{8,72},{9... | collective-permute-start | bytes 1572872 | tf_op jit(solution)/shard_map/ppermute | solution.py:248
  26.9 10.5 %collective-permute-done.2.refs_3_ = f32[1024,128]{1,0:T(8,128)S(1)} collective-permute-done((f32[1024,128]{1,0:T(8,128)S(1)}, f32[1024,128]{1,0:T(8,128)S(1)}, u32[]{:S(2)}, u32[]{:S(2)}) %collective-permute-start.2) | collective-permute-done | bytes 524320 | tf_op jit(solution)/shard_map/ppermute | solution.py:248
  37.4 4.2 %collective-permute-start.29 = (f32[512,128]{1,0:T(8,128)S(1)}, f32[512,128]{1,0:T(8,128)S(1)}, u32[]{:S(2)}, u32[]{:S(2)}) collective-permute-start(f32[512,128]{1,0:T(8,128)S(1)} %get-tuple-element.42), channel_id=1, source_target_pairs={{0,1},{1,0},{2,3},{3,2},{4,5},{5,4},{6,7},{7,6},{8,9},{9,8},{10,11... | collective-permute-start | bytes 786440 | tf_op jit(solution)/shard_map/ppermute | solution.py:36
  41.6 4.2 %collective-permute-start.3 = (f32[1024,128]{1,0:T(8,128)S(1)}, f32[1024,128]{1,0:T(8,128)}, u32[]{:S(2)}, u32[]{:S(2)}) collective-permute-start(f32[1024,128]{1,0:T(8,128)S(1)} %collective-permute-done.2.refs_3_), channel_id=1, source_target_pairs={{0,2},{1,3},{2,4},{3,5},{4,6},{5,7},{6,0},{7,1},{8,10},{9,11},{10,... | collective-permute-start | bytes 1572872 | tf_op jit(solution)/shard_map/ppermute | solution.py:28
  47.3 2.7 %collective-permute-start.30 = (f32[1024,128]{1,0:T(8,128)}, f32[1024,128]{1,0:T(8,128)}, u32[]{:S(2)}, u32[]{:S(2)}) collective-permute-start(f32[1024,128]{1,0:T(8,128)} %pad_maximum_fusion.3), channel_id=1, source_target_pairs={{0,112},{16,0},{32,16},{48,32},{64,48},{80,64},{96,80},{112,96},{1... | collective-permute-start | bytes 1572872 | tf_op jit(solution)/shard_map/ppermute | solution.py:44
  50.0 3.1 %pick_tiles.2.mine = f32[512,512]{1,0:T(8,128)} custom-call(s32[6,4]{1,0:T(8,128)} %get-tuple-element.48.place, f32[1024,1024]{1,0:T(8,128)} %ancestor.3), custom_call_target="tpu_custom_call" | custom-call | flops 262144 | bytes 2097152 | tf_op jit(solution)/shard_map/pick_tiles/pallas_call | solution.py:91
  54.1 3.6 %collective-permute-done.3.refs_0_ = f32[1024,128]{1,0:T(8,128)} collective-permute-done((f32[1024,128]{1,0:T(8,128)S(1)}, f32[1024,128]{1,0:T(8,128)}, u32[]{:S(2)}, u32[]{:S(2)}) %collective-permute-start.3) | collective-permute-done | bytes 524320 | tf_op jit(solution)/shard_map/ppermute | solution.py:28
  59.0 3.9 %collective-permute-done.30 = f32[1024,128]{1,0:T(8,128)} collective-permute-done((f32[1024,128]{1,0:T(8,128)}, f32[1024,128]{1,0:T(8,128)}, u32[]{:S(2)}, u32[]{:S(2)}) %collective-permute-start.30) | collective-permute-done | bytes 524320 | tf_op jit(solution)/shard_map/ppermute | solution.py:44
  64.1 2.8 %collective-permute-done.6.refs_1_ = f32[1024,128]{1,0:T(8,128)S(1)} collective-permute-done((f32[1024,128]{1,0:T(8,128)}, f32[1024,128]{1,0:T(8,128)S(1)}, u32[]{:S(2)}, u32[]{:S(2)}) %collective-permute-start.6) | collective-permute-done | bytes 524320 | tf_op jit(solution)/shard_map/ppermute | solution.py:28
  67.8 2.7 %collective-permute-done.7.refs_2_ = f32[1024,128]{1,0:T(8,128)S(1)} collective-permute-done((f32[1024,128]{1,0:T(8,128)}, f32[1024,128]{1,0:T(8,128)S(1)}, u32[]{:S(2)}, u32[]{:S(2)}) %collective-permute-start.7) | collective-permute-done | bytes 524320 | tf_op jit(solution)/shard_map/ppermute | solution.py:32
  74.3 2.7 %collective-permute-done.33 = f32[1024,128]{1,0:T(8,128)} collective-permute-done((f32[1024,128]{1,0:T(8,128)}, f32[1024,128]{1,0:T(8,128)}, u32[]{:S(2)}, u32[]{:S(2)}) %collective-permute-start.33) | collective-permute-done | bytes 524320 | tf_op jit(solution)/shard_map/ppermute | solution.py:44
  79.5 4.7 %split_tiles.1 = (bf16[1024,1024]{1,0:T(8,128)(2,1)}, bf16[1024,1024]{1,0:T(8,128)(2,1)}) custom-call(f32[512,512]{1,0:T(8,128)} %pick_tiles.2.mine, f32[512,512]{1,0:T(8,128)} %copy-done.3, f32[512,512]{1,0:T(8,128)} %copy-done.4, f32[512,512]{1,0:T(8,128)} %collective-permute-done.12.sibling_partner), custom_call_target="tpu_custom_call" | custom-call | flops 3145728 | bytes 8388608 | tf_op jit(solution)/shard_map/split_tiles/pallas_call | solution.py:124
  84.7 8.2 %partial_products.2.refs_7_ = f32[8,128,1024]{2,1,0:T(8,128)} custom-call(s32[5]{0:T(128)} %stack.50.where, f32[1024,128]{1,0:T(8,128)} %collective-permute-done.3.refs_0_, f32[1024,128]{1,0:T(8,128)} %collective-permute-done.13.refs_1_, f32[1024,128]{1,0:T(8,128)} %collective-permute-done.5.refs_2_, f32[1024,128]{1,0:T(8,128)} %copy-done.9, ...), custom_call_target="tpu_custom_call" | custom-call | flops 3221225472 | bytes 8388608 | tf_op jit(solution)/shard_map/partial_products/pallas_call | solution.py:196
  93.6 8.2 %partial_products.3 = f32[8,128,1024]{2,1,0:T(8,128)} custom-call(s32[5]{0:T(128)} %stack.50.where, f32[1024,128]{1,0:T(8,128)} %collective-permute-done.4.refs_0_, f32[1024,128]{1,0:T(8,128)} %copy-done.1, f32[1024,128]{1,0:T(8,128)} %copy-done.2, f32[512,128]{1,0:T(8,128)} %collective-permute-done.8.refs_3_, ...), custom_call_target="tpu_custom_call", output_to_operand_aliasing={{}: (8, {})} | custom-call | flops 3221225472 | bytes 8388608 | tf_op jit(solution)/shard_map/partial_products/pallas_call | solution.py:196
  105.1 2.7 %collective-permute-start.32 = (f32[1024,128]{1,0:T(8,128)}, f32[1024,128]{1,0:T(8,128)S(1)}, u32[]{:S(2)}, u32[]{:S(2)}) collective-permute-start(f32[1024,128]{1,0:T(8,128)} %collective-permute-done.31), channel_id=1, source_target_pairs={{0,112},{16,0},{32,16},{48,32},{64,48},{80,64},{96,80},{112,96},{1... | collective-permute-start | bytes 1572872 | tf_op jit(solution)/shard_map/ppermute | solution.py:44
  108.6 2.9 %collective-permute-start.19 = (f32[64,1024]{1,0:T(8,128)S(1)}, f32[64,1024]{1,0:T(8,128)S(1)}, u32[]{:S(2)}, u32[]{:S(2)}) collective-permute-start(f32[64,1024]{1,0:T(8,128)S(1)} %get-tuple-element.32), channel_id=1, source_target_pairs={{0,112},{16,0},{32,16},{48,32},{64,48},{80,64},{96,80},{112,96},{1... | collective-permute-start | bytes 786440 | tf_op jit(solution)/shard_map/ppermute | solution.py:44
  112.7 2.7 %collective-permute-start.17 = (f32[64,1024]{1,0:T(8,128)S(1)}, f32[64,1024]{1,0:T(8,128)S(1)}, u32[]{:S(2)}, u32[]{:S(2)}) collective-permute-start(f32[64,1024]{1,0:T(8,128)S(1)} %get-tuple-element.36), channel_id=1, source_target_pairs={{0,112},{16,0},{32,16},{48,32},{64,48},{80,64},{96,80},{112,96},{1... | collective-permute-start | bytes 786440 | tf_op jit(solution)/shard_map/ppermute | solution.py:44
  116.6 8.6 %collective-permute-done.19 = f32[64,1024]{1,0:T(8,128)S(1)} collective-permute-done((f32[64,1024]{1,0:T(8,128)S(1)}, f32[64,1024]{1,0:T(8,128)S(1)}, u32[]{:S(2)}, u32[]{:S(2)}) %collective-permute-start.19) | collective-permute-done | bytes 262176 | tf_op jit(solution)/shard_map/ppermute | solution.py:44
  126.1 2.9 %collective-permute-start.23 = (f32[64,1024]{1,0:T(8,128)S(1)}, f32[64,1024]{1,0:T(8,128)S(1)}, u32[]{:S(2)}, u32[]{:S(2)}) collective-permute-start(f32[64,1024]{1,0:T(8,128)S(1)} %get-tuple-element.30), channel_id=1, source_target_pairs={{0,112},{16,0},{32,16},{48,32},{64,48},{80,64},{96,80},{112,96},{1... | collective-permute-start | bytes 786440 | tf_op jit(solution)/shard_map/ppermute | solution.py:44
  131.5 2.9 %collective-permute-start.21 = (f32[64,1024]{1,0:T(8,128)S(1)}, f32[64,1024]{1,0:T(8,128)S(1)}, u32[]{:S(2)}, u32[]{:S(2)}) collective-permute-start(f32[64,1024]{1,0:T(8,128)S(1)} %get-tuple-element.28), channel_id=1, source_target_pairs={{0,112},{16,0},{32,16},{48,32},{64,48},{80,64},{96,80},{112,96},{1... | collective-permute-start | bytes 786440 | tf_op jit(solution)/shard_map/ppermute | solution.py:44
  138.8 2.7 %collective-permute-start.25 = (f32[64,1024]{1,0:T(8,128)S(1)}, f32[64,1024]{1,0:T(8,128)S(1)}, u32[]{:S(2)}, u32[]{:S(2)}) collective-permute-start(f32[64,1024]{1,0:T(8,128)S(1)} %get-tuple-element.26), channel_id=1, source_target_pairs={{0,112},{16,0},{32,16},{48,32},{64,48},{80,64},{96,80},{112,96},{1... | collective-permute-start | bytes 786440 | tf_op jit(solution)/shard_map/ppermute | solution.py:44
  141.5 2.8 %collective-permute-done.20 = f32[64,1024]{1,0:T(8,128)S(1)} collective-permute-done((f32[64,1024]{1,0:T(8,128)S(1)}, f32[64,1024]{1,0:T(8,128)S(1)}, u32[]{:S(2)}, u32[]{:S(2)}) %collective-permute-start.20) | collective-permute-done | bytes 262176 | tf_op jit(solution)/shard_map/ppermute | solution.py:44
  144.5 3.2 %collective-permute-done.37 = f32[512,128]{1,0:T(8,128)S(1)} collective-permute-done((f32[512,128]{1,0:T(8,128)S(1)}, f32[512,128]{1,0:T(8,128)S(1)}, u32[]{:S(2)}, u32[]{:S(2)}) %collective-permute-start.37) | collective-permute-done | bytes 262176 | tf_op jit(solution)/shard_map/ppermute | solution.py:44
  147.7 2.3 %collective-permute-done.36 = f32[512,128]{1,0:T(8,128)S(1)} collective-permute-done((f32[512,128]{1,0:T(8,128)S(1)}, f32[512,128]{1,0:T(8,128)S(1)}, u32[]{:S(2)}, u32[]{:S(2)}) %collective-permute-start.36) | collective-permute-done | bytes 262176 | tf_op jit(solution)/shard_map/ppermute | solution.py:44
  150.1 3.2 %collective-permute-done.25 = f32[64,1024]{1,0:T(8,128)S(1)} collective-permute-done((f32[64,1024]{1,0:T(8,128)S(1)}, f32[64,1024]{1,0:T(8,128)S(1)}, u32[]{:S(2)}, u32[]{:S(2)}) %collective-permute-start.25) | collective-permute-done | bytes 262176 | tf_op jit(solution)/shard_map/ppermute | solution.py:44
  158.7 2.5 %collective-permute-done.26 = f32[64,1024]{1,0:T(8,128)S(1)} collective-permute-done((f32[64,1024]{1,0:T(8,128)S(1)}, f32[64,1024]{1,0:T(8,128)S(1)}, u32[]{:S(2)}, u32[]{:S(2)}) %collective-permute-start.26) | collective-permute-done | bytes 262176 | tf_op jit(solution)/shard_map/ppermute | solution.py:44
  161.3 8.2 %collective-permute-start.28 = (f32[128,1024]{1,0:T(8,128)S(1)}, f32[128,1024]{1,0:T(8,128)S(1)}, u32[]{:S(2)}, u32[]{:S(2)}) collective-permute-start(f32[128,1024]{1,0:T(8,128)S(1)} %pad_maximum_fusion.1), channel_id=1, source_target_pairs={{0,1},{1,0},{2,3},{3,2},{4,5},{5,4},{6,7},{7,6},{8,9},{9,8},{10,11... | collective-permute-start | bytes 1572872 | tf_op jit(solution)/shard_map/ppermute | solution.py:36
  174.3 5.4 %all-to-all-start = ((f32[8,256,128]{2,1,0:T(8,128)}), f32[8,256,128]{2,1,0:T(8,128)S(1)}, u32[]{:S(2)}, u32[]{:S(2)}) async-start(f32[8,256,128]{2,1,0:T(8,128)} %pad_maximum_fusion), calls=%async_computation | async-start | bytes 2097152 | tf_op jit(solution)/shard_map/all_to_all | solution.py:275
  180.6 13.7 %all-to-all-done = f32[8,256,128]{2,1,0:T(8,128)S(1)} async-done(((f32[8,256,128]{2,1,0:T(8,128)}), f32[8,256,128]{2,1,0:T(8,128)S(1)}, u32[]{:S(2)}, u32[]{:S(2)}) %all-to-all-start) | async-done | bytes 1048608 | tf_op jit(solution)/shard_map/all_to_all | solution.py:275
  (113 shorter events, 46.2 us)
Async XLA Ops:
  1.8 16.1 %collective-permute-start.1 = (f32[512,128]{1,0:T(8,128)S(1)}, f32[512,128]{1,0:T(8,128)S(1)}, u32[]{:S(2)}, u32[]{:S(2)}) collective-permute-start(f32[512,128]{1,0:T(8,128)S(1)} %get-tuple-element.44), channel_id=1, source_target_pairs={{0,9},{1,11},{2,13},{3,15},{4,1},{5,3},{6,5},{7,7},{8,0},{9,2},{10... | collective-permute-start | bytes 786440 | tf_op jit(solution)/shard_map/ppermute | solution.py:237
  6.5 11.3 %collective-permute-start = (f32[512,128]{1,0:T(8,128)S(1)}, f32[512,128]{1,0:T(8,128)S(1)}, u32[]{:S(2)}, u32[]{:S(2)}) collective-permute-start(f32[512,128]{1,0:T(8,128)S(1)} %get-tuple-element.43), channel_id=1, source_target_pairs={{0,0},{1,2},{2,4},{3,6},{4,8},{5,10},{6,12},{7,14},{8,9},{9,11},{1... | collective-permute-start | bytes 786440 | tf_op jit(solution)/shard_map/ppermute | solution.py:236
  15.1 38.8 %collective-permute-start.10 = (f32[512,512]{1,0:T(8,128)}, f32[512,512]{1,0:T(8,128)S(1)}, u32[]{:S(2)}, u32[]{:S(2)}) collective-permute-start(f32[512,512]{1,0:T(8,128)} %pick_tiles.3), channel_id=1, source_target_pairs={{0,128},{128,0},{1,129},{129,1},{2,130},{130,2},{3,131},{131,3},{4... | collective-permute-start | bytes 3145736 | tf_op jit(solution)/shard_map/ppermute | solution.py:40
  17.9 19.5 %collective-permute-start.2 = (f32[1024,128]{1,0:T(8,128)S(1)}, f32[1024,128]{1,0:T(8,128)S(1)}, u32[]{:S(2)}, u32[]{:S(2)}) collective-permute-start(f32[1024,128]{1,0:T(8,128)S(1)} %pad_maximum_fusion.2), channel_id=1, source_target_pairs={{0,0},{1,65},{2,18},{3,83},{4,36},{5,101},{6,54},{7,119},{8,72},{9... | collective-permute-start | bytes 1572872 | tf_op jit(solution)/shard_map/ppermute | solution.py:248
  37.4 16.6 %collective-permute-start.5 = (f32[1024,128]{1,0:T(8,128)S(1)}, f32[1024,128]{1,0:T(8,128)}, u32[]{:S(2)}, u32[]{:S(2)}) collective-permute-start(f32[1024,128]{1,0:T(8,128)S(1)} %collective-permute-done.2.refs_3_), channel_id=1, source_target_pairs={{0,8},{1,9},{2,10},{3,11},{4,12},{5,13},{6,14},{7,15},{8,0},{9,1},... | collective-permute-start | bytes 1572872 | tf_op jit(solution)/shard_map/ppermute | solution.py:32
  41.6 16.1 %collective-permute-start.3 = (f32[1024,128]{1,0:T(8,128)S(1)}, f32[1024,128]{1,0:T(8,128)}, u32[]{:S(2)}, u32[]{:S(2)}) collective-permute-start(f32[1024,128]{1,0:T(8,128)S(1)} %collective-permute-done.2.refs_3_), channel_id=1, source_target_pairs={{0,2},{1,3},{2,4},{3,5},{4,6},{5,7},{6,0},{7,1},{8,10},{9,11},{10,... | collective-permute-start | bytes 1572872 | tf_op jit(solution)/shard_map/ppermute | solution.py:28
  47.3 15.6 %collective-permute-start.30 = (f32[1024,128]{1,0:T(8,128)}, f32[1024,128]{1,0:T(8,128)}, u32[]{:S(2)}, u32[]{:S(2)}) collective-permute-start(f32[1024,128]{1,0:T(8,128)} %pad_maximum_fusion.3), channel_id=1, source_target_pairs={{0,112},{16,0},{32,16},{48,32},{64,48},{80,64},{96,80},{112,96},{1... | collective-permute-start | bytes 1572872 | tf_op jit(solution)/shard_map/ppermute | solution.py:44
  53.1 24.4 %collective-permute-start.11 = (f32[512,512]{1,0:T(8,128)}, f32[512,512]{1,0:T(8,128)S(1)}, u32[]{:S(2)}, u32[]{:S(2)}) collective-permute-start(f32[512,512]{1,0:T(8,128)} %pick_tiles.2.mine), channel_id=1, source_target_pairs={{0,1},{1,0},{2,3},{3,2},{4,5},{5,4},{6,7},{7,6},{8,9},{9,8},{10,11... | collective-permute-start | bytes 3145736 | tf_op jit(solution)/shard_map/ppermute | solution.py:36
  53.9 24.7 %collective-permute-start.12 = (f32[512,512]{1,0:T(8,128)S(1)}, f32[512,512]{1,0:T(8,128)}, u32[]{:S(2)}, u32[]{:S(2)}) collective-permute-start(f32[512,512]{1,0:T(8,128)S(1)} %collective-permute-done.10.partner), channel_id=1, source_target_pairs={{0,1},{1,0},{2,3},{3,2},{4,5},{5,4},{6,7},{7,6},{8,9},{9,8},{10,11... | collective-permute-start | bytes 3145736 | tf_op jit(solution)/shard_map/ppermute | solution.py:36
  54.0 12.9 %collective-permute-start.6 = (f32[1024,128]{1,0:T(8,128)}, f32[1024,128]{1,0:T(8,128)S(1)}, u32[]{:S(2)}, u32[]{:S(2)}) collective-permute-start(f32[1024,128]{1,0:T(8,128)} %collective-permute-done.5.refs_2_), channel_id=1, source_target_pairs={{0,6},{1,7},{2,0},{3,1},{4,2},{5,3},{6,4},{7,5},{8,14},{9,15},{10,... | collective-permute-start | bytes 1572872 | tf_op jit(solution)/shard_map/ppermute | solution.py:28
  57.7 12.8 %collective-permute-start.7 = (f32[1024,128]{1,0:T(8,128)}, f32[1024,128]{1,0:T(8,128)S(1)}, u32[]{:S(2)}, u32[]{:S(2)}) collective-permute-start(f32[1024,128]{1,0:T(8,128)} %collective-permute-done.3.refs_0_), channel_id=1, source_target_pairs={{0,8},{1,9},{2,10},{3,11},{4,12},{5,13},{6,14},{7,15},{8,0},{9,1},... | collective-permute-start | bytes 1572872 | tf_op jit(solution)/shard_map/ppermute | solution.py:32
  62.9 14.1 %collective-permute-start.33 = (f32[1024,128]{1,0:T(8,128)}, f32[1024,128]{1,0:T(8,128)}, u32[]{:S(2)}, u32[]{:S(2)}) collective-permute-start(f32[1024,128]{1,0:T(8,128)} %pad_maximum_fusion.3), channel_id=1, source_target_pairs={{0,16},{16,32},{32,48},{48,64},{64,80},{80,96},{96,112},{112,0},{1... | collective-permute-start | bytes 1572872 | tf_op jit(solution)/shard_map/ppermute | solution.py:44
  66.9 17.3 %collective-permute-start.13 = (f32[1024,128]{1,0:T(8,128)}, f32[1024,128]{1,0:T(8,128)}, u32[]{:S(2)}, u32[]{:S(2)}) collective-permute-start(f32[1024,128]{1,0:T(8,128)} %copy-done.9), channel_id=1, source_target_pairs={{0,6},{1,7},{2,0},{3,1},{4,2},{5,3},{6,4},{7,5},{8,14},{9,15},{10,... | collective-permute-start | bytes 1572872 | tf_op jit(solution)/shard_map/ppermute | solution.py:28
  70.5 22.4 %collective-permute-start.4 = (f32[1024,128]{1,0:T(8,128)}, f32[1024,128]{1,0:T(8,128)}, u32[]{:S(2)}, u32[]{:S(2)}) collective-permute-start(f32[1024,128]{1,0:T(8,128)} %collective-permute-done.3.refs_0_), channel_id=1, source_target_pairs={{0,2},{1,3},{2,4},{3,5},{4,6},{5,7},{6,0},{7,1},{8,10},{9,11},{10,... | collective-permute-start | bytes 1572872 | tf_op jit(solution)/shard_map/ppermute | solution.py:28
  77.1 28.1 %collective-permute-start.31 = (f32[1024,128]{1,0:T(8,128)}, f32[1024,128]{1,0:T(8,128)}, u32[]{:S(2)}, u32[]{:S(2)}) collective-permute-start(f32[1024,128]{1,0:T(8,128)} %collective-permute-done.30), channel_id=1, source_target_pairs={{0,112},{16,0},{32,16},{48,32},{64,48},{80,64},{96,80},{112,96},{1... | collective-permute-start | bytes 1572872 | tf_op jit(solution)/shard_map/ppermute | solution.py:44
  77.6 35.2 %collective-permute-start.34 = (f32[1024,128]{1,0:T(8,128)}, f32[1024,128]{1,0:T(8,128)}, u32[]{:S(2)}, u32[]{:S(2)}) collective-permute-start(f32[1024,128]{1,0:T(8,128)} %collective-permute-done.33), channel_id=1, source_target_pairs={{0,16},{16,32},{32,48},{48,64},{64,80},{80,96},{96,112},{112,0},{1... | collective-permute-start | bytes 1572872 | tf_op jit(solution)/shard_map/ppermute | solution.py:44
  78.5 14.4 %collective-permute-start.8 = (f32[512,128]{1,0:T(8,128)}, f32[512,128]{1,0:T(8,128)}, u32[]{:S(2)}, u32[]{:S(2)}) collective-permute-start(f32[512,128]{1,0:T(8,128)} %slice.113), channel_id=1, source_target_pairs={{0,2},{1,3},{2,4},{3,5},{4,6},{5,7},{6,0},{7,1},{8,10},{9,11},{10,... | collective-permute-start | bytes 786440 | tf_op jit(solution)/shard_map/ppermute | solution.py:28
  105.1 26.3 %collective-permute-start.32 = (f32[1024,128]{1,0:T(8,128)}, f32[1024,128]{1,0:T(8,128)S(1)}, u32[]{:S(2)}, u32[]{:S(2)}) collective-permute-start(f32[1024,128]{1,0:T(8,128)} %collective-permute-done.31), channel_id=1, source_target_pairs={{0,112},{16,0},{32,16},{48,32},{64,48},{80,64},{96,80},{112,96},{1... | collective-permute-start | bytes 1572872 | tf_op jit(solution)/shard_map/ppermute | solution.py:44
  108.6 16.6 %collective-permute-start.19 = (f32[64,1024]{1,0:T(8,128)S(1)}, f32[64,1024]{1,0:T(8,128)S(1)}, u32[]{:S(2)}, u32[]{:S(2)}) collective-permute-start(f32[64,1024]{1,0:T(8,128)S(1)} %get-tuple-element.32), channel_id=1, source_target_pairs={{0,112},{16,0},{32,16},{48,32},{64,48},{80,64},{96,80},{112,96},{1... | collective-permute-start | bytes 786440 | tf_op jit(solution)/shard_map/ppermute | solution.py:44
  112.6 13.5 %collective-permute-start.15 = (f32[64,1024]{1,0:T(8,128)S(1)}, f32[64,1024]{1,0:T(8,128)S(1)}, u32[]{:S(2)}, u32[]{:S(2)}) collective-permute-start(f32[64,1024]{1,0:T(8,128)S(1)} %get-tuple-element.37), channel_id=1, source_target_pairs={{0,16},{16,32},{32,48},{48,64},{64,80},{80,96},{96,112},{112,0},{1... | collective-permute-start | bytes 786440 | tf_op jit(solution)/shard_map/ppermute | solution.py:44
  112.7 18.1 %collective-permute-start.17 = (f32[64,1024]{1,0:T(8,128)S(1)}, f32[64,1024]{1,0:T(8,128)S(1)}, u32[]{:S(2)}, u32[]{:S(2)}) collective-permute-start(f32[64,1024]{1,0:T(8,128)S(1)} %get-tuple-element.36), channel_id=1, source_target_pairs={{0,112},{16,0},{32,16},{48,32},{64,48},{80,64},{96,80},{112,96},{1... | collective-permute-start | bytes 786440 | tf_op jit(solution)/shard_map/ppermute | solution.py:44
  116.6 18.9 %collective-permute-start.35 = (f32[1024,128]{1,0:T(8,128)}, f32[1024,128]{1,0:T(8,128)S(1)}, u32[]{:S(2)}, u32[]{:S(2)}) collective-permute-start(f32[1024,128]{1,0:T(8,128)} %collective-permute-done.34), channel_id=1, source_target_pairs={{0,16},{16,32},{32,48},{48,64},{64,80},{80,96},{96,112},{112,0},{1... | collective-permute-start | bytes 1572872 | tf_op jit(solution)/shard_map/ppermute | solution.py:44
  125.3 13.4 %collective-permute-start.22 = (f32[64,1024]{1,0:T(8,128)S(1)}, f32[64,1024]{1,0:T(8,128)S(1)}, u32[]{:S(2)}, u32[]{:S(2)}) collective-permute-start(f32[64,1024]{1,0:T(8,128)S(1)} %get-tuple-element.31), channel_id=1, source_target_pairs={{0,16},{16,32},{32,48},{48,64},{64,80},{80,96},{96,112},{112,0},{1... | collective-permute-start | bytes 786440 | tf_op jit(solution)/shard_map/ppermute | solution.py:44
  126.1 12.6 %collective-permute-start.23 = (f32[64,1024]{1,0:T(8,128)S(1)}, f32[64,1024]{1,0:T(8,128)S(1)}, u32[]{:S(2)}, u32[]{:S(2)}) collective-permute-start(f32[64,1024]{1,0:T(8,128)S(1)} %get-tuple-element.30), channel_id=1, source_target_pairs={{0,112},{16,0},{32,16},{48,32},{64,48},{80,64},{96,80},{112,96},{1... | collective-permute-start | bytes 786440 | tf_op jit(solution)/shard_map/ppermute | solution.py:44
  130.9 13.4 %collective-permute-start.20 = (f32[64,1024]{1,0:T(8,128)S(1)}, f32[64,1024]{1,0:T(8,128)S(1)}, u32[]{:S(2)}, u32[]{:S(2)}) collective-permute-start(f32[64,1024]{1,0:T(8,128)S(1)} %get-tuple-element.29), channel_id=1, source_target_pairs={{0,16},{16,32},{32,48},{48,64},{64,80},{80,96},{96,112},{112,0},{1... | collective-permute-start | bytes 786440 | tf_op jit(solution)/shard_map/ppermute | solution.py:44
  131.5 12.8 %collective-permute-start.21 = (f32[64,1024]{1,0:T(8,128)S(1)}, f32[64,1024]{1,0:T(8,128)S(1)}, u32[]{:S(2)}, u32[]{:S(2)}) collective-permute-start(f32[64,1024]{1,0:T(8,128)S(1)} %get-tuple-element.28), channel_id=1, source_target_pairs={{0,112},{16,0},{32,16},{48,32},{64,48},{80,64},{96,80},{112,96},{1... | collective-permute-start | bytes 786440 | tf_op jit(solution)/shard_map/ppermute | solution.py:44
  135.5 12.2 %collective-permute-start.37 = (f32[512,128]{1,0:T(8,128)S(1)}, f32[512,128]{1,0:T(8,128)S(1)}, u32[]{:S(2)}, u32[]{:S(2)}) collective-permute-start(f32[512,128]{1,0:T(8,128)S(1)} %slice.135), channel_id=1, source_target_pairs={{0,112},{16,0},{32,16},{48,32},{64,48},{80,64},{96,80},{112,96},{1... | collective-permute-start | bytes 786440 | tf_op jit(solution)/shard_map/ppermute | solution.py:44
  138.7 11.2 %collective-permute-start.36 = (f32[512,128]{1,0:T(8,128)S(1)}, f32[512,128]{1,0:T(8,128)S(1)}, u32[]{:S(2)}, u32[]{:S(2)}) collective-permute-start(f32[512,128]{1,0:T(8,128)S(1)} %slice.134), channel_id=1, source_target_pairs={{0,16},{16,32},{32,48},{48,64},{64,80},{80,96},{96,112},{112,0},{1... | collective-permute-start | bytes 786440 | tf_op jit(solution)/shard_map/ppermute | solution.py:44
  138.8 14.5 %collective-permute-start.25 = (f32[64,1024]{1,0:T(8,128)S(1)}, f32[64,1024]{1,0:T(8,128)S(1)}, u32[]{:S(2)}, u32[]{:S(2)}) collective-permute-start(f32[64,1024]{1,0:T(8,128)S(1)} %get-tuple-element.26), channel_id=1, source_target_pairs={{0,112},{16,0},{32,16},{48,32},{64,48},{80,64},{96,80},{112,96},{1... | collective-permute-start | bytes 786440 | tf_op jit(solution)/shard_map/ppermute | solution.py:44
  144.4 11.2 %collective-permute-start.24 = (f32[64,1024]{1,0:T(8,128)S(1)}, f32[64,1024]{1,0:T(8,128)S(1)}, u32[]{:S(2)}, u32[]{:S(2)}) collective-permute-start(f32[64,1024]{1,0:T(8,128)S(1)} %fusion.10), channel_id=1, source_target_pairs={{0,16},{16,32},{32,48},{48,64},{64,80},{80,96},{96,112},{112,0},{1... | collective-permute-start | bytes 786440 | tf_op jit(solution)/shard_map/ppermute | solution.py:44
  150.0 11.2 %collective-permute-start.26 = (f32[64,1024]{1,0:T(8,128)S(1)}, f32[64,1024]{1,0:T(8,128)S(1)}, u32[]{:S(2)}, u32[]{:S(2)}) collective-permute-start(f32[64,1024]{1,0:T(8,128)S(1)} %get-tuple-element.27), channel_id=1, source_target_pairs={{0,16},{16,32},{32,48},{48,64},{64,80},{80,96},{96,112},{112,0},{1... | collective-permute-start | bytes 786440 | tf_op jit(solution)/shard_map/ppermute | solution.py:44
  174.3 20.0 %all-to-all-start = ((f32[8,256,128]{2,1,0:T(8,128)}), f32[8,256,128]{2,1,0:T(8,128)S(1)}, u32[]{:S(2)}, u32[]{:S(2)}) async-start(f32[8,256,128]{2,1,0:T(8,128)} %pad_maximum_fusion), calls=%async_computation | async-start | bytes 2097152 | tf_op jit(solution)/shard_map/all_to_all | solution.py:275
  (17 other events, 204.4 us)
where the time goes:
time: 198 us; the launch traced here: 195 us
  starting transfers between devices  75.7 us (38%)
  waiting for transfers between devices  69.3 us (35%)
  Pallas kernels  27.2 us (14%)
  local copies, waits for them, and re-layouts  12 us (6%)
  other arithmetic  7.19 us (4%)
  matrix products  2.59 us (1%)
    ppermute x22, waiting for transfers between devices, along_z(): return lax.ppermute(value, 'col', [(z, (z + step) % Z) for z in range(Z)])  35.9 us
    ppermute x22, starting transfers between devices, along_z(): return lax.ppermute(value, 'col', [(z, (z + step) % Z) for z in range(Z)])  29 us
    pallas_call x2, Pallas kernels, partial_products(): pl.pallas_call(functools.partial(partial_kernel, spots, len(blocks) == co...  16.4 us
    all_to_all x1, waiting for transfers between devices, scattered_in_plane(): lax.all_to_all(terms, ('col', 'row'), 0, 0, axis_index_groups=groups, til...  13.7 us
    ppermute x4, starting transfers between devices, across_core(): return lax.ppermute(value, 'row', row_pairs(lambda y, x, c: (y, x, 1 - c)))  13.2 us
    ppermute x1, waiting for transfers between devices, mirrored(): return lax.ppermute(value, ('col', 'row'), pairs)  10.5 us
    ppermute x1, starting transfers between devices, mirrored(): return lax.ppermute(value, ('col', 'row'), pairs)  8.99 us
    ppermute x6, starting transfers between devices, along_x(): lax.ppermute(value, 'row', row_pairs(lambda y, x, c: (y, x + step, c)))  8.34 us
  transfers between devices with their start and end apart: 39, of which 19 were waited for; matrix products, arithmetic and copies ran while one was open for 8% of the time, Pallas kernels for 14%

commit v1 on v0

--- a/solution.py
+++ b/solution.py
@@ -101,6 +101,7 @@
         cost_estimate=pl.CostEstimate(
             flops=edge * edge, bytes_accessed=8 * edge * edge, transcendentals=0
         ),
+        compiler_params=pltpu.CompilerParams(vmem_limit_bytes=6 * 2**20),
         name="pick_tiles",
     )(place, ancestor)
 
@@ -125,6 +126,7 @@
         split_kernel,
         out_shape=(shape, shape),
         cost_estimate=pl.CostEstimate(flops=12 * edge * edge, bytes_accessed=32 * edge * edge, transcendentals=0),
+        compiler_params=pltpu.CompilerParams(vmem_limit_bytes=20 * 2**20),
         name="split_tiles",
     )(*tiles)
 
@@ -132,10 +134,9 @@
 STEP = 512
 
 
-def partial_kernel(spots, whole, where, *refs):
+def partial_kernel(spots, where, *refs):
     count = len(spots)
-    taken = count + (not whole)
-    blocks, (high, low) = refs[:taken], refs[taken : taken + 2]
+    blocks, (high, low) = refs[:count], refs[count : count + 2]
     parts, block_high, block_low, total, sems = refs[-5:]
     edge = SLOTS * TILE
     k = pl.program_id(0)
@@ -145,11 +146,8 @@
     def _():
         for j in range(count):
             for half in range(2):
-                if whole or j < count - 1:
-                    start = pl.multiple_of((half ^ flip) * edge, edge)
-                    value = blocks[j][pl.ds(start, edge), :]
-                else:
-                    value = jnp.where(flip == 0, blocks[j + half][...], blocks[j + 1 - half][...])
+                start = pl.multiple_of((half ^ flip) * edge, edge)
+                value = blocks[j][pl.ds(start, edge), :]
                 spot = (pl.ds(j * TILE, TILE), pl.ds(half * edge, edge))
                 block_high[spot], block_low[spot] = two_terms(value.T)
 
@@ -194,7 +192,7 @@
         args.append(parts)
     rows = count * TILE
     return pl.pallas_call(
-        functools.partial(partial_kernel, spots, len(blocks) == count),
+        functools.partial(partial_kernel, spots),
         grid_spec=pltpu.PrefetchScalarGridSpec(
             num_scalar_prefetch=1,
             grid=(steps,),
@@ -214,6 +212,7 @@
             bytes_accessed=4 * edge * (4 * edge + 4 * rows),
             transcendentals=0,
         ),
+        compiler_params=pltpu.CompilerParams(vmem_limit_bytes=24 * 2**20),
         name="partial_products",
     )(*args)
 
@@ -315,23 +314,18 @@
     left = along_x(own_columns, 1)
     right = along_x(own_columns, -1)
     over = across_y(own_columns)
+    far = along_x(own_columns, 2)
     up2 = along_z(up1, 1)
     down2 = along_z(down1, -1)
-    far = along_x(left, 1)
+    over_left = along_x(over, 1)
     over_right = along_x(over, -1)
-    over_left = across_y(left)
+    corner = across_y(far)
     up3 = along_z(up2, 1)
     down3 = along_z(down2, -1)
-    half = SLOTS * TILE
-    spots = ((0, 3), (0, 1), (1, 0), (0, 0))
-    parts = placed(spots, [left, right, over, own_columns])
-    far_a = along_x(over_left[:half], 1)
-    far_b = along_x(over_right[half:], -1)
-    up4 = along_z(up3[:half], 1)
-    down4 = along_z(down3[half:], -1)
-    z_far = jnp.concatenate([up4, down4], axis=0)
-    spots = ((0, 2), (1, 1), (1, 3), (1, 2))
-    parts = placed(spots, [far, over_right, over_left, far_a, far_b], parts)
+    parts = placed(((0, 3), (0, 1), (0, 2), (0, 0)), [left, right, far, own_columns])
+    z_far = along_z(up3, 1)
+    spots = ((1, 0), (1, 1), (1, 3), (1, 2))
+    parts = placed(spots, [over, over_right, over_left, corner], parts)
     rows_full = jnp.stack([own_rows, down1, down2, down3, z_far, up3, up2, up1])
     reduced = scattered_along_z(parts)
 

time: 198 us -> 212 us (1.071)
  starting transfers between devices: 75.7 us -> 104 us
  Pallas kernels: 27.2 us -> 17.1 us
  other arithmetic: 7.19 us -> 4.25 us
  local copies, waits for them, and re-layouts: 12 us -> 9.16 us
  waiting for transfers between devices: 69.3 us -> 71.5 us
    ppermute x22 -> x21, starting transfers between devices: 29 us -> 51.1 us  [along_z(): return lax.ppermute(value, 'col', [(z, (z + step) % Z) for z in range(Z)])]
    ppermute x1, waiting for transfers between devices: 10.5 us -> 0.01 us  [mirrored(): return lax.ppermute(value, ('col', 'row'), pairs)]
    ppermute x6 -> x5, starting transfers between devices: 8.34 us -> 16 us  [along_x(): lax.ppermute(value, 'row', row_pairs(lambda y, x, c: (y, x + step, c)))]
    ppermute x22 -> x21, waiting for transfers between devices: 35.9 us -> 43 us  [along_z(): return lax.ppermute(value, 'col', [(z, (z + step) % Z) for z in range(Z)])]
    ppermute x6 -> x5, waiting for transfers between devices: 6.45 us -> 13.2 us  [along_x(): lax.ppermute(value, 'row', row_pairs(lambda y, x, c: (y, x + step, c)))]
    ppermute x4, starting transfers between devices: 13.2 us -> 6.92 us  [across_core(): return lax.ppermute(value, 'row', row_pairs(lambda y, x, c: (y, x, 1 - c)))]
    pallas_call x1, Pallas kernels: 4.67 us -> 0.56 us  [split_tiles(): pl.pallas_call(split_kernel, out_shape=(shape, shape), cost_estimate=pl.C...]
    ppermute x1, starting transfers between devices: 8.99 us -> 12.6 us  [mirrored(): return lax.ppermute(value, ('col', 'row'), pairs)]
  transfers between devices with their start and end apart: 39 -> 37, of which waited for: 19 -> 16; matrix products, arithmetic and copies ran while one was open for 8% -> 2% of each run, Pallas kernels for 14% -> 7%
where the time goes in v1:
time: 212 us; the launch traced here: 209 us
  starting transfers between devices  104 us (49%)
  waiting for transfers between devices  71.5 us (34%)
  Pallas kernels  17.1 us (8%)
  local copies, waits for them, and re-layouts  9.16 us (4%)
  other arithmetic  4.25 us (2%)
  matrix products  2.59 us (1%)
    ppermute x21, starting transfers between devices, along_z(): return lax.ppermute(value, 'col', [(z, (z + step) % Z) for z in range(Z)])  51.1 us
    ppermute x21, waiting for transfers between devices, along_z(): return lax.ppermute(value, 'col', [(z, (z + step) % Z) for z in range(Z)])  43 us
    ppermute x5, starting transfers between devices, along_x(): lax.ppermute(value, 'row', row_pairs(lambda y, x, c: (y, x + step, c)))  16 us
    all_to_all x1, waiting for transfers between devices, scattered_in_plane(): lax.all_to_all(terms, ('col', 'row'), 0, 0, axis_index_groups=groups, til...  13.4 us
    ppermute x5, waiting for transfers between devices, along_x(): lax.ppermute(value, 'row', row_pairs(lambda y, x, c: (y, x + step, c)))  13.2 us
    pallas_call x2, Pallas kernels, partial_products(): pl.pallas_call(functools.partial(partial_kernel, spots), grid_spec=pltpu....  13.2 us
    ppermute x1, starting transfers between devices, mirrored(): return lax.ppermute(value, ('col', 'row'), pairs)  12.6 us
    all_to_all x1, starting transfers between devices, scattered_in_plane(): lax.all_to_all(terms, ('col', 'row'), 0, 0, axis_index_groups=groups, til...  7.22 us
  transfers between devices with their start and end apart: 37, of which 16 were waited for; matrix products, arithmetic and copies ran while one was open for 2% of the time, Pallas kernels for 7%

profile of v1, /device:TPU:3, one launch (start us, length us, event | category | flops | bytes accessed | tf_op | source)
XLA Modules:
  0.0 209.2 jit_solution(9077593911763690346)
XLA Ops:
  3.6 2.2 %copy-done = f32[1024,1024]{1,0:T(8,128)S(1)} copy-done((f32[1024,1024]{1,0:T(8,128)S(1)}, f32[1024,1024]{1,0:T(8,128)}, u32[]{:S(2)}) %copy-start) | copy-done | bytes 4194328
  5.7 2.2 %pick_tiles.3 = f32[512,512]{1,0:T(8,128)} custom-call(s32[6,4]{1,0:T(8,128)S(1)} %get-tuple-element.47.place, f32[1024,1024]{1,0:T(8,128)S(1)} %copy-done), custom_call_target="tpu_custom_call" | custom-call | flops 262144 | bytes 2097152 | tf_op jit(solution)/shard_map/pick_tiles/pallas_call | solution.py:91
  8.0 3.0 %collective-permute-start.8 = (f32[512,512]{1,0:T(8,128)}, f32[512,512]{1,0:T(8,128)S(1)}, u32[]{:S(2)}, u32[]{:S(2)}) collective-permute-start(f32[512,512]{1,0:T(8,128)} %pick_tiles.3), channel_id=1, source_target_pairs={{0,128},{128,0},{1,129},{129,1},{2,130},{130,2},{3,131},{131,3},{4... | collective-permute-start | bytes 3145736 | tf_op jit(solution)/shard_map/ppermute | solution.py:40
  11.0 3.8 %collective-permute-start.1 = (f32[512,128]{1,0:T(8,128)S(1)}, f32[512,128]{1,0:T(8,128)S(1)}, u32[]{:S(2)}, u32[]{:S(2)}) collective-permute-start(f32[512,128]{1,0:T(8,128)S(1)} %get-tuple-element.44), channel_id=1, source_target_pairs={{0,9},{1,11},{2,13},{3,15},{4,1},{5,3},{6,5},{7,7},{8,0},{9,2},{10... | collective-permute-start | bytes 786440 | tf_op jit(solution)/shard_map/ppermute | solution.py:236
  14.9 2.6 %collective-permute-start = (f32[512,128]{1,0:T(8,128)S(1)}, f32[512,128]{1,0:T(8,128)S(1)}, u32[]{:S(2)}, u32[]{:S(2)}) collective-permute-start(f32[512,128]{1,0:T(8,128)S(1)} %get-tuple-element.43), channel_id=1, source_target_pairs={{0,0},{1,2},{2,4},{3,6},{4,8},{5,10},{6,12},{7,14},{8,9},{9,11},{1... | collective-permute-start | bytes 786440 | tf_op jit(solution)/shard_map/ppermute | solution.py:235
  23.2 12.6 %collective-permute-start.2 = (f32[1024,128]{1,0:T(8,128)S(1)}, f32[1024,128]{1,0:T(8,128)}, u32[]{:S(2)}, u32[]{:S(2)}) collective-permute-start(f32[1024,128]{1,0:T(8,128)S(1)} %pad_maximum_fusion.2), channel_id=1, source_target_pairs={{0,0},{1,65},{2,18},{3,83},{4,36},{5,101},{6,54},{7,119},{8,72},{9... | collective-permute-start | bytes 1572872 | tf_op jit(solution)/shard_map/ppermute | solution.py:247
  35.9 12.3 %collective-permute-start.29 = (f32[1024,128]{1,0:T(8,128)S(1)}, f32[1024,128]{1,0:T(8,128)S(1)}, u32[]{:S(2)}, u32[]{:S(2)}) collective-permute-start(f32[1024,128]{1,0:T(8,128)S(1)} %pad_maximum_fusion.3), channel_id=1, source_target_pairs={{0,112},{16,0},{32,16},{48,32},{64,48},{80,64},{96,80},{112,96},{1... | collective-permute-start | bytes 1572872 | tf_op jit(solution)/shard_map/ppermute | solution.py:44
  49.5 14.8 %collective-permute-done.29 = f32[1024,128]{1,0:T(8,128)S(1)} collective-permute-done((f32[1024,128]{1,0:T(8,128)S(1)}, f32[1024,128]{1,0:T(8,128)S(1)}, u32[]{:S(2)}, u32[]{:S(2)}) %collective-permute-start.29) | collective-permute-done | bytes 524320 | tf_op jit(solution)/shard_map/ppermute | solution.py:44
  64.3 3.5 %collective-permute-start.6 = (f32[1024,128]{1,0:T(8,128)}, f32[1024,128]{1,0:T(8,128)}, u32[]{:S(2)}, u32[]{:S(2)}) collective-permute-start(f32[1024,128]{1,0:T(8,128)} %collective-permute-done.2.refs_3_), channel_id=1, source_target_pairs={{0,4},{1,5},{2,6},{3,7},{4,0},{5,1},{6,2},{7,3},{8,12},{9,13},{10,... | collective-permute-start | bytes 1572872 | tf_op jit(solution)/shard_map/ppermute | solution.py:28
  67.8 2.2 %collective-permute-start.11 = (f32[1024,128]{1,0:T(8,128)}, f32[1024,128]{1,0:T(8,128)}, u32[]{:S(2)}, u32[]{:S(2)}) collective-permute-start(f32[1024,128]{1,0:T(8,128)} %collective-permute-done.2.refs_3_), channel_id=1, source_target_pairs={{0,2},{1,3},{2,4},{3,5},{4,6},{5,7},{6,0},{7,1},{8,10},{9,11},{10,... | collective-permute-start | bytes 1572872 | tf_op jit(solution)/shard_map/ppermute | solution.py:28
  70.0 2.2 %collective-permute-start.12 = (f32[1024,128]{1,0:T(8,128)}, f32[1024,128]{1,0:T(8,128)}, u32[]{:S(2)}, u32[]{:S(2)}) collective-permute-start(f32[1024,128]{1,0:T(8,128)} %collective-permute-done.2.refs_3_), channel_id=1, source_target_pairs={{0,6},{1,7},{2,0},{3,1},{4,2},{5,3},{6,4},{7,5},{8,14},{9,15},{10,... | collective-permute-start | bytes 1572872 | tf_op jit(solution)/shard_map/ppermute | solution.py:28
  72.2 2.6 %collective-permute-start.4 = (f32[1024,128]{1,0:T(8,128)}, f32[1024,128]{1,0:T(8,128)}, u32[]{:S(2)}, u32[]{:S(2)}) collective-permute-start(f32[1024,128]{1,0:T(8,128)} %collective-permute-done.3.refs_0_), channel_id=1, source_target_pairs={{0,6},{1,7},{2,0},{3,1},{4,2},{5,3},{6,4},{7,5},{8,14},{9,15},{10,... | collective-permute-start | bytes 1572872 | tf_op jit(solution)/shard_map/ppermute | solution.py:28
  74.8 5.1 %collective-permute-done.6.refs_2_ = f32[1024,128]{1,0:T(8,128)} collective-permute-done((f32[1024,128]{1,0:T(8,128)}, f32[1024,128]{1,0:T(8,128)}, u32[]{:S(2)}, u32[]{:S(2)}) %collective-permute-start.6) | collective-permute-done | bytes 524320 | tf_op jit(solution)/shard_map/ppermute | solution.py:28
  79.9 5.5 %collective-permute-start.5 = (f32[1024,128]{1,0:T(8,128)}, f32[1024,128]{1,0:T(8,128)}, u32[]{:S(2)}, u32[]{:S(2)}) collective-permute-start(f32[1024,128]{1,0:T(8,128)} %collective-permute-done.3.refs_0_), channel_id=1, source_target_pairs={{0,2},{1,3},{2,4},{3,5},{4,6},{5,7},{6,0},{7,1},{8,10},{9,11},{10,... | collective-permute-start | bytes 1572872 | tf_op jit(solution)/shard_map/ppermute | solution.py:28
  88.3 7.4 %collective-permute-done.11.refs_0_ = f32[1024,128]{1,0:T(8,128)} collective-permute-done((f32[1024,128]{1,0:T(8,128)}, f32[1024,128]{1,0:T(8,128)}, u32[]{:S(2)}, u32[]{:S(2)}) %collective-permute-start.11) | collective-permute-done | bytes 524320 | tf_op jit(solution)/shard_map/ppermute | solution.py:28
  97.2 6.6 %partial_products.2.refs_6_ = f32[8,128,1024]{2,1,0:T(8,128)S(1)} custom-call(s32[5]{0:T(128)S(1)} %stack.50.where, f32[1024,128]{1,0:T(8,128)} %collective-permute-done.11.refs_0_, f32[1024,128]{1,0:T(8,128)} %collective-permute-done.12.refs_1_, f32[1024,128]{1,0:T(8,128)} %collective-permute-done.6.refs_2_, f32[1024,128]{1,0:T(8,128)} %collective-permute-done.2.refs_3_, ...), custom_call_target="tpu_custom_call" | custom-call | flops 3221225472 | bytes 8388608 | tf_op jit(solution)/shard_map/partial_products/pallas_call | solution.py:194
  104.6 6.6 %partial_products.3 = f32[8,128,1024]{2,1,0:T(8,128)S(1)} custom-call(s32[5]{0:T(128)S(1)} %stack.50.where, f32[1024,128]{1,0:T(8,128)} %collective-permute-done.3.refs_0_, f32[1024,128]{1,0:T(8,128)} %collective-permute-done.4.refs_1_, f32[1024,128]{1,0:T(8,128)} %collective-permute-done.5.refs_2_, ...), custom_call_target="tpu_custom_call", output_to_operand_aliasing={{}: (7, {})} | custom-call | flops 3221225472 | bytes 8388608 | tf_op jit(solution)/shard_map/partial_products/pallas_call | solution.py:194
  112.9 3.6 %collective-permute-start.34 = (f32[1024,128]{1,0:T(8,128)S(1)}, f32[1024,128]{1,0:T(8,128)S(1)}, u32[]{:S(2)}, u32[]{:S(2)}) collective-permute-start(f32[1024,128]{1,0:T(8,128)S(1)} %collective-permute-done.33), channel_id=1, source_target_pairs={{0,16},{16,32},{32,48},{48,64},{64,80},{80,96},{96,112},{112,0},{1... | collective-permute-start | bytes 1572872 | tf_op jit(solution)/shard_map/ppermute | solution.py:44
  116.5 2.7 %collective-permute-start.17 = (f32[64,1024]{1,0:T(8,128)S(1)}, f32[64,1024]{1,0:T(8,128)S(1)}, u32[]{:S(2)}, u32[]{:S(2)}) collective-permute-start(f32[64,1024]{1,0:T(8,128)S(1)} %get-tuple-element.33), channel_id=1, source_target_pairs={{0,16},{16,32},{32,48},{48,64},{64,80},{80,96},{96,112},{112,0},{1... | collective-permute-start | bytes 786440 | tf_op jit(solution)/shard_map/ppermute | solution.py:44
  120.1 2.7 %collective-permute-start.14 = (f32[64,1024]{1,0:T(8,128)S(1)}, f32[64,1024]{1,0:T(8,128)S(1)}, u32[]{:S(2)}, u32[]{:S(2)}) collective-permute-start(f32[64,1024]{1,0:T(8,128)S(1)} %get-tuple-element.37), channel_id=1, source_target_pairs={{0,16},{16,32},{32,48},{48,64},{64,80},{80,96},{96,112},{112,0},{1... | collective-permute-start | bytes 786440 | tf_op jit(solution)/shard_map/ppermute | solution.py:44
  122.9 13.3 %collective-permute-done.17 = f32[64,1024]{1,0:T(8,128)S(1)} collective-permute-done((f32[64,1024]{1,0:T(8,128)S(1)}, f32[64,1024]{1,0:T(8,128)S(1)}, u32[]{:S(2)}, u32[]{:S(2)}) %collective-permute-start.17) | collective-permute-done | bytes 262176 | tf_op jit(solution)/shard_map/ppermute | solution.py:44
  138.7 3.1 %collective-permute-done.14 = f32[64,1024]{1,0:T(8,128)S(1)} collective-permute-done((f32[64,1024]{1,0:T(8,128)S(1)}, f32[64,1024]{1,0:T(8,128)S(1)}, u32[]{:S(2)}, u32[]{:S(2)}) %collective-permute-start.14) | collective-permute-done | bytes 262176 | tf_op jit(solution)/shard_map/ppermute | solution.py:44
  147.5 2.3 %collective-permute-start.35 = (f32[1024,128]{1,0:T(8,128)S(1)}, f32[1024,128]{1,0:T(8,128)S(1)}, u32[]{:S(2)}, u32[]{:S(2)}) collective-permute-start(f32[1024,128]{1,0:T(8,128)S(1)} %collective-permute-done.34), channel_id=1, source_target_pairs={{0,16},{16,32},{32,48},{48,64},{64,80},{80,96},{96,112},{112,0},{1... | collective-permute-start | bytes 1572872 | tf_op jit(solution)/shard_map/ppermute | solution.py:44
  152.0 4.2 %collective-permute-done.20 = f32[64,1024]{1,0:T(8,128)S(1)} collective-permute-done((f32[64,1024]{1,0:T(8,128)S(1)}, f32[64,1024]{1,0:T(8,128)S(1)}, u32[]{:S(2)}, u32[]{:S(2)}) %collective-permute-start.20) | collective-permute-done | bytes 262176 | tf_op jit(solution)/shard_map/ppermute | solution.py:44
  156.2 8.7 %collective-permute-start.23 = (f32[64,1024]{1,0:T(8,128)S(1)}, f32[64,1024]{1,0:T(8,128)S(1)}, u32[]{:S(2)}, u32[]{:S(2)}) collective-permute-start(f32[64,1024]{1,0:T(8,128)S(1)} %fusion.9), channel_id=1, source_target_pairs={{0,16},{16,32},{32,48},{48,64},{64,80},{80,96},{96,112},{112,0},{1... | collective-permute-start | bytes 786440 | tf_op jit(solution)/shard_map/ppermute | solution.py:44
  165.0 3.5 %collective-permute-start.25 = (f32[64,1024]{1,0:T(8,128)S(1)}, f32[64,1024]{1,0:T(8,128)S(1)}, u32[]{:S(2)}, u32[]{:S(2)}) collective-permute-start(f32[64,1024]{1,0:T(8,128)S(1)} %get-tuple-element.27), channel_id=1, source_target_pairs={{0,16},{16,32},{32,48},{48,64},{64,80},{80,96},{96,112},{112,0},{1... | collective-permute-start | bytes 786440 | tf_op jit(solution)/shard_map/ppermute | solution.py:44
  169.5 3.2 %collective-permute-start.26 = (f32[64,1024]{1,0:T(8,128)S(1)}, f32[64,1024]{1,0:T(8,128)S(1)}, u32[]{:S(2)}, u32[]{:S(2)}) collective-permute-start(f32[64,1024]{1,0:T(8,128)S(1)} %get-tuple-element.25), channel_id=1, source_target_pairs={{0,112},{16,0},{32,16},{48,32},{64,48},{80,64},{96,80},{112,96},{1... | collective-permute-start | bytes 786440 | tf_op jit(solution)/shard_map/ppermute | solution.py:44
  172.8 2.2 %collective-permute-done.25 = f32[64,1024]{1,0:T(8,128)S(1)} collective-permute-done((f32[64,1024]{1,0:T(8,128)S(1)}, f32[64,1024]{1,0:T(8,128)S(1)}, u32[]{:S(2)}, u32[]{:S(2)}) %collective-permute-start.25) | collective-permute-done | bytes 262176 | tf_op jit(solution)/shard_map/ppermute | solution.py:44
  175.1 2.6 %collective-permute-done.26 = f32[64,1024]{1,0:T(8,128)S(1)} collective-permute-done((f32[64,1024]{1,0:T(8,128)S(1)}, f32[64,1024]{1,0:T(8,128)S(1)}, u32[]{:S(2)}, u32[]{:S(2)}) %collective-permute-start.26) | collective-permute-done | bytes 262176 | tf_op jit(solution)/shard_map/ppermute | solution.py:44
  177.7 5.2 %collective-permute-start.27 = (f32[128,1024]{1,0:T(8,128)S(1)}, f32[128,1024]{1,0:T(8,128)S(1)}, u32[]{:S(2)}, u32[]{:S(2)}) collective-permute-start(f32[128,1024]{1,0:T(8,128)S(1)} %pad_maximum_fusion.1), channel_id=1, source_target_pairs={{0,1},{1,0},{2,3},{3,2},{4,5},{5,4},{6,7},{7,6},{8,9},{9,8},{10,11... | collective-permute-start | bytes 1572872 | tf_op jit(solution)/shard_map/ppermute | solution.py:36
  186.9 7.2 %all-to-all-start = ((f32[8,256,128]{2,1,0:T(8,128)}), f32[8,256,128]{2,1,0:T(8,128)S(1)}, u32[]{:S(2)}, u32[]{:S(2)}) async-start(f32[8,256,128]{2,1,0:T(8,128)} %pad_maximum_fusion), calls=%async_computation | async-start | bytes 2097152 | tf_op jit(solution)/shard_map/all_to_all | solution.py:274
  195.0 13.4 %all-to-all-done = f32[8,256,128]{2,1,0:T(8,128)S(1)} async-done(((f32[8,256,128]{2,1,0:T(8,128)}), f32[8,256,128]{2,1,0:T(8,128)S(1)}, u32[]{:S(2)}, u32[]{:S(2)}) %all-to-all-start) | async-done | bytes 1048608 | tf_op jit(solution)/shard_map/all_to_all | solution.py:274
  (109 shorter events, 35.0 us)
Async XLA Ops:
  8.0 40.2 %collective-permute-start.8 = (f32[512,512]{1,0:T(8,128)}, f32[512,512]{1,0:T(8,128)S(1)}, u32[]{:S(2)}, u32[]{:S(2)}) collective-permute-start(f32[512,512]{1,0:T(8,128)} %pick_tiles.3), channel_id=1, source_target_pairs={{0,128},{128,0},{1,129},{129,1},{2,130},{130,2},{3,131},{131,3},{4... | collective-permute-start | bytes 3145736 | tf_op jit(solution)/shard_map/ppermute | solution.py:40
  11.0 10.6 %collective-permute-start.1 = (f32[512,128]{1,0:T(8,128)S(1)}, f32[512,128]{1,0:T(8,128)S(1)}, u32[]{:S(2)}, u32[]{:S(2)}) collective-permute-start(f32[512,128]{1,0:T(8,128)S(1)} %get-tuple-element.44), channel_id=1, source_target_pairs={{0,9},{1,11},{2,13},{3,15},{4,1},{5,3},{6,5},{7,7},{8,0},{9,2},{10... | collective-permute-start | bytes 786440 | tf_op jit(solution)/shard_map/ppermute | solution.py:236
  17.5 18.3 %collective-permute-start.28 = (f32[512,128]{1,0:T(8,128)S(1)}, f32[512,128]{1,0:T(8,128)S(1)}, u32[]{:S(2)}, u32[]{:S(2)}) collective-permute-start(f32[512,128]{1,0:T(8,128)S(1)} %get-tuple-element.42), channel_id=1, source_target_pairs={{0,1},{1,0},{2,3},{3,2},{4,5},{5,4},{6,7},{7,6},{8,9},{9,8},{10,11... | collective-permute-start | bytes 786440 | tf_op jit(solution)/shard_map/ppermute | solution.py:36
  21.0 49.0 %collective-permute-start.9 = (f32[512,512]{1,0:T(8,128)S(1)}, f32[512,512]{1,0:T(8,128)S(1)}, u32[]{:S(2)}, u32[]{:S(2)}) collective-permute-start(f32[512,512]{1,0:T(8,128)S(1)} %pick_tiles.2.mine), channel_id=1, source_target_pairs={{0,1},{1,0},{2,3},{3,2},{4,5},{5,4},{6,7},{7,6},{8,9},{9,8},{10,11... | collective-permute-start | bytes 3145736 | tf_op jit(solution)/shard_map/ppermute | solution.py:36
  23.2 26.0 %collective-permute-start.2 = (f32[1024,128]{1,0:T(8,128)S(1)}, f32[1024,128]{1,0:T(8,128)}, u32[]{:S(2)}, u32[]{:S(2)}) collective-permute-start(f32[1024,128]{1,0:T(8,128)S(1)} %pad_maximum_fusion.2), channel_id=1, source_target_pairs={{0,0},{1,65},{2,18},{3,83},{4,36},{5,101},{6,54},{7,119},{8,72},{9... | collective-permute-start | bytes 1572872 | tf_op jit(solution)/shard_map/ppermute | solution.py:247
  35.9 28.4 %collective-permute-start.29 = (f32[1024,128]{1,0:T(8,128)S(1)}, f32[1024,128]{1,0:T(8,128)S(1)}, u32[]{:S(2)}, u32[]{:S(2)}) collective-permute-start(f32[1024,128]{1,0:T(8,128)S(1)} %pad_maximum_fusion.3), channel_id=1, source_target_pairs={{0,112},{16,0},{32,16},{48,32},{64,48},{80,64},{96,80},{112,96},{1... | collective-permute-start | bytes 1572872 | tf_op jit(solution)/shard_map/ppermute | solution.py:44
  48.2 37.2 %collective-permute-start.10 = (f32[512,512]{1,0:T(8,128)S(1)}, f32[512,512]{1,0:T(8,128)S(1)}, u32[]{:S(2)}, u32[]{:S(2)}) collective-permute-start(f32[512,512]{1,0:T(8,128)S(1)} %collective-permute-done.8.partner), channel_id=1, source_target_pairs={{0,1},{1,0},{2,3},{3,2},{4,5},{5,4},{6,7},{7,6},{8,9},{9,8},{10,11... | collective-permute-start | bytes 3145736 | tf_op jit(solution)/shard_map/ppermute | solution.py:36
  49.2 18.5 %collective-permute-start.32 = (f32[1024,128]{1,0:T(8,128)S(1)}, f32[1024,128]{1,0:T(8,128)S(1)}, u32[]{:S(2)}, u32[]{:S(2)}) collective-permute-start(f32[1024,128]{1,0:T(8,128)S(1)} %pad_maximum_fusion.3), channel_id=1, source_target_pairs={{0,16},{16,32},{32,48},{48,64},{64,80},{80,96},{96,112},{112,0},{1... | collective-permute-start | bytes 1572872 | tf_op jit(solution)/shard_map/ppermute | solution.py:44
  49.3 22.9 %collective-permute-start.3 = (f32[1024,128]{1,0:T(8,128)}, f32[1024,128]{1,0:T(8,128)}, u32[]{:S(2)}, u32[]{:S(2)}) collective-permute-start(f32[1024,128]{1,0:T(8,128)} %collective-permute-done.2.refs_3_), channel_id=1, source_target_pairs={{0,8},{1,9},{2,10},{3,11},{4,12},{5,13},{6,14},{7,15},{8,0},{9,1},... | collective-permute-start | bytes 1572872 | tf_op jit(solution)/shard_map/ppermute | solution.py:32
  64.3 15.6 %collective-permute-start.6 = (f32[1024,128]{1,0:T(8,128)}, f32[1024,128]{1,0:T(8,128)}, u32[]{:S(2)}, u32[]{:S(2)}) collective-permute-start(f32[1024,128]{1,0:T(8,128)} %collective-permute-done.2.refs_3_), channel_id=1, source_target_pairs={{0,4},{1,5},{2,6},{3,7},{4,0},{5,1},{6,2},{7,3},{8,12},{9,13},{10,... | collective-permute-start | bytes 1572872 | tf_op jit(solution)/shard_map/ppermute | solution.py:28
  67.8 28.0 %collective-permute-start.11 = (f32[1024,128]{1,0:T(8,128)}, f32[1024,128]{1,0:T(8,128)}, u32[]{:S(2)}, u32[]{:S(2)}) collective-permute-start(f32[1024,128]{1,0:T(8,128)} %collective-permute-done.2.refs_3_), channel_id=1, source_target_pairs={{0,2},{1,3},{2,4},{3,5},{4,6},{5,7},{6,0},{7,1},{8,10},{9,11},{10,... | collective-permute-start | bytes 1572872 | tf_op jit(solution)/shard_map/ppermute | solution.py:28
  70.0 25.8 %collective-permute-start.12 = (f32[1024,128]{1,0:T(8,128)}, f32[1024,128]{1,0:T(8,128)}, u32[]{:S(2)}, u32[]{:S(2)}) collective-permute-start(f32[1024,128]{1,0:T(8,128)} %collective-permute-done.2.refs_3_), channel_id=1, source_target_pairs={{0,6},{1,7},{2,0},{3,1},{4,2},{5,3},{6,4},{7,5},{8,14},{9,15},{10,... | collective-permute-start | bytes 1572872 | tf_op jit(solution)/shard_map/ppermute | solution.py:28
  72.2 31.7 %collective-permute-start.4 = (f32[1024,128]{1,0:T(8,128)}, f32[1024,128]{1,0:T(8,128)}, u32[]{:S(2)}, u32[]{:S(2)}) collective-permute-start(f32[1024,128]{1,0:T(8,128)} %collective-permute-done.3.refs_0_), channel_id=1, source_target_pairs={{0,6},{1,7},{2,0},{3,1},{4,2},{5,3},{6,4},{7,5},{8,14},{9,15},{10,... | collective-permute-start | bytes 1572872 | tf_op jit(solution)/shard_map/ppermute | solution.py:28
  79.9 24.7 %collective-permute-start.5 = (f32[1024,128]{1,0:T(8,128)}, f32[1024,128]{1,0:T(8,128)}, u32[]{:S(2)}, u32[]{:S(2)}) collective-permute-start(f32[1024,128]{1,0:T(8,128)} %collective-permute-done.3.refs_0_), channel_id=1, source_target_pairs={{0,2},{1,3},{2,4},{3,5},{4,6},{5,7},{6,0},{7,1},{8,10},{9,11},{10,... | collective-permute-start | bytes 1572872 | tf_op jit(solution)/shard_map/ppermute | solution.py:28
  86.4 18.1 %collective-permute-start.7 = (f32[1024,128]{1,0:T(8,128)}, f32[1024,128]{1,0:T(8,128)}, u32[]{:S(2)}, u32[]{:S(2)}) collective-permute-start(f32[1024,128]{1,0:T(8,128)} %collective-permute-done.6.refs_2_), channel_id=1, source_target_pairs={{0,8},{1,9},{2,10},{3,11},{4,12},{5,13},{6,14},{7,15},{8,0},{9,1},... | collective-permute-start | bytes 1572872 | tf_op jit(solution)/shard_map/ppermute | solution.py:32
  95.8 27.0 %collective-permute-start.30 = (f32[1024,128]{1,0:T(8,128)}, f32[1024,128]{1,0:T(8,128)S(1)}, u32[]{:S(2)}, u32[]{:S(2)}) collective-permute-start(f32[1024,128]{1,0:T(8,128)} %copy-done.8), channel_id=1, source_target_pairs={{0,112},{16,0},{32,16},{48,32},{64,48},{80,64},{96,80},{112,96},{1... | collective-permute-start | bytes 1572872 | tf_op jit(solution)/shard_map/ppermute | solution.py:44
  95.8 17.1 %collective-permute-start.33 = (f32[1024,128]{1,0:T(8,128)}, f32[1024,128]{1,0:T(8,128)S(1)}, u32[]{:S(2)}, u32[]{:S(2)}) collective-permute-start(f32[1024,128]{1,0:T(8,128)} %copy-done.6), channel_id=1, source_target_pairs={{0,16},{16,32},{32,48},{48,64},{64,80},{80,96},{96,112},{112,0},{1... | collective-permute-start | bytes 1572872 | tf_op jit(solution)/shard_map/ppermute | solution.py:44
  112.9 31.6 %collective-permute-start.34 = (f32[1024,128]{1,0:T(8,128)S(1)}, f32[1024,128]{1,0:T(8,128)S(1)}, u32[]{:S(2)}, u32[]{:S(2)}) collective-permute-start(f32[1024,128]{1,0:T(8,128)S(1)} %collective-permute-done.33), channel_id=1, source_target_pairs={{0,16},{16,32},{32,48},{48,64},{64,80},{80,96},{96,112},{112,0},{1... | collective-permute-start | bytes 1572872 | tf_op jit(solution)/shard_map/ppermute | solution.py:44
  116.5 19.6 %collective-permute-start.17 = (f32[64,1024]{1,0:T(8,128)S(1)}, f32[64,1024]{1,0:T(8,128)S(1)}, u32[]{:S(2)}, u32[]{:S(2)}) collective-permute-start(f32[64,1024]{1,0:T(8,128)S(1)} %get-tuple-element.33), channel_id=1, source_target_pairs={{0,16},{16,32},{32,48},{48,64},{64,80},{80,96},{96,112},{112,0},{1... | collective-permute-start | bytes 786440 | tf_op jit(solution)/shard_map/ppermute | solution.py:44
  119.2 18.5 %collective-permute-start.18 = (f32[64,1024]{1,0:T(8,128)S(1)}, f32[64,1024]{1,0:T(8,128)S(1)}, u32[]{:S(2)}, u32[]{:S(2)}) collective-permute-start(f32[64,1024]{1,0:T(8,128)S(1)} %get-tuple-element.32), channel_id=1, source_target_pairs={{0,112},{16,0},{32,16},{48,32},{64,48},{80,64},{96,80},{112,96},{1... | collective-permute-start | bytes 786440 | tf_op jit(solution)/shard_map/ppermute | solution.py:44
  120.1 21.7 %collective-permute-start.14 = (f32[64,1024]{1,0:T(8,128)S(1)}, f32[64,1024]{1,0:T(8,128)S(1)}, u32[]{:S(2)}, u32[]{:S(2)}) collective-permute-start(f32[64,1024]{1,0:T(8,128)S(1)} %get-tuple-element.37), channel_id=1, source_target_pairs={{0,16},{16,32},{32,48},{48,64},{64,80},{80,96},{96,112},{112,0},{1... | collective-permute-start | bytes 786440 | tf_op jit(solution)/shard_map/ppermute | solution.py:44
  122.8 20.6 %collective-permute-start.16 = (f32[64,1024]{1,0:T(8,128)S(1)}, f32[64,1024]{1,0:T(8,128)S(1)}, u32[]{:S(2)}, u32[]{:S(2)}) collective-permute-start(f32[64,1024]{1,0:T(8,128)S(1)} %get-tuple-element.36), channel_id=1, source_target_pairs={{0,112},{16,0},{32,16},{48,32},{64,48},{80,64},{96,80},{112,96},{1... | collective-permute-start | bytes 786440 | tf_op jit(solution)/shard_map/ppermute | solution.py:44
  136.2 28.8 %collective-permute-start.31 = (f32[1024,128]{1,0:T(8,128)S(1)}, f32[1024,128]{1,0:T(8,128)S(1)}, u32[]{:S(2)}, u32[]{:S(2)}) collective-permute-start(f32[1024,128]{1,0:T(8,128)S(1)} %collective-permute-done.30), channel_id=1, source_target_pairs={{0,112},{16,0},{32,16},{48,32},{64,48},{80,64},{96,80},{112,96},{1... | collective-permute-start | bytes 1572872 | tf_op jit(solution)/shard_map/ppermute | solution.py:44
  137.8 9.6 %collective-permute-start.21 = (f32[64,1024]{1,0:T(8,128)S(1)}, f32[64,1024]{1,0:T(8,128)S(1)}, u32[]{:S(2)}, u32[]{:S(2)}) collective-permute-start(f32[64,1024]{1,0:T(8,128)S(1)} %get-tuple-element.31), channel_id=1, source_target_pairs={{0,16},{16,32},{32,48},{48,64},{64,80},{80,96},{96,112},{112,0},{1... | collective-permute-start | bytes 786440 | tf_op jit(solution)/shard_map/ppermute | solution.py:44
  141.8 8.8 %collective-permute-start.22 = (f32[64,1024]{1,0:T(8,128)S(1)}, f32[64,1024]{1,0:T(8,128)S(1)}, u32[]{:S(2)}, u32[]{:S(2)}) collective-permute-start(f32[64,1024]{1,0:T(8,128)S(1)} %get-tuple-element.30), channel_id=1, source_target_pairs={{0,112},{16,0},{32,16},{48,32},{64,48},{80,64},{96,80},{112,96},{1... | collective-permute-start | bytes 786440 | tf_op jit(solution)/shard_map/ppermute | solution.py:44
  143.5 8.5 %collective-permute-start.19 = (f32[64,1024]{1,0:T(8,128)S(1)}, f32[64,1024]{1,0:T(8,128)S(1)}, u32[]{:S(2)}, u32[]{:S(2)}) collective-permute-start(f32[64,1024]{1,0:T(8,128)S(1)} %get-tuple-element.29), channel_id=1, source_target_pairs={{0,16},{16,32},{32,48},{48,64},{64,80},{80,96},{96,112},{112,0},{1... | collective-permute-start | bytes 786440 | tf_op jit(solution)/shard_map/ppermute | solution.py:44
  144.5 11.6 %collective-permute-start.20 = (f32[64,1024]{1,0:T(8,128)S(1)}, f32[64,1024]{1,0:T(8,128)S(1)}, u32[]{:S(2)}, u32[]{:S(2)}) collective-permute-start(f32[64,1024]{1,0:T(8,128)S(1)} %get-tuple-element.28), channel_id=1, source_target_pairs={{0,112},{16,0},{32,16},{48,32},{64,48},{80,64},{96,80},{112,96},{1... | collective-permute-start | bytes 786440 | tf_op jit(solution)/shard_map/ppermute | solution.py:44
  147.5 17.5 %collective-permute-start.35 = (f32[1024,128]{1,0:T(8,128)S(1)}, f32[1024,128]{1,0:T(8,128)S(1)}, u32[]{:S(2)}, u32[]{:S(2)}) collective-permute-start(f32[1024,128]{1,0:T(8,128)S(1)} %collective-permute-done.34), channel_id=1, source_target_pairs={{0,16},{16,32},{32,48},{48,64},{64,80},{80,96},{96,112},{112,0},{1... | collective-permute-start | bytes 1572872 | tf_op jit(solution)/shard_map/ppermute | solution.py:44
  150.6 17.9 %collective-permute-start.24 = (f32[64,1024]{1,0:T(8,128)S(1)}, f32[64,1024]{1,0:T(8,128)S(1)}, u32[]{:S(2)}, u32[]{:S(2)}) collective-permute-start(f32[64,1024]{1,0:T(8,128)S(1)} %get-tuple-element.26), channel_id=1, source_target_pairs={{0,112},{16,0},{32,16},{48,32},{64,48},{80,64},{96,80},{112,96},{1... | collective-permute-start | bytes 786440 | tf_op jit(solution)/shard_map/ppermute | solution.py:44
  156.2 13.2 %collective-permute-start.23 = (f32[64,1024]{1,0:T(8,128)S(1)}, f32[64,1024]{1,0:T(8,128)S(1)}, u32[]{:S(2)}, u32[]{:S(2)}) collective-permute-start(f32[64,1024]{1,0:T(8,128)S(1)} %fusion.9), channel_id=1, source_target_pairs={{0,16},{16,32},{32,48},{48,64},{64,80},{80,96},{96,112},{112,0},{1... | collective-permute-start | bytes 786440 | tf_op jit(solution)/shard_map/ppermute | solution.py:44
  165.0 10.0 %collective-permute-start.25 = (f32[64,1024]{1,0:T(8,128)S(1)}, f32[64,1024]{1,0:T(8,128)S(1)}, u32[]{:S(2)}, u32[]{:S(2)}) collective-permute-start(f32[64,1024]{1,0:T(8,128)S(1)} %get-tuple-element.27), channel_id=1, source_target_pairs={{0,16},{16,32},{32,48},{48,64},{64,80},{80,96},{96,112},{112,0},{1... | collective-permute-start | bytes 786440 | tf_op jit(solution)/shard_map/ppermute | solution.py:44
  186.9 21.5 %all-to-all-start = ((f32[8,256,128]{2,1,0:T(8,128)}), f32[8,256,128]{2,1,0:T(8,128)S(1)}, u32[]{:S(2)}, u32[]{:S(2)}) async-start(f32[8,256,128]{2,1,0:T(8,128)} %pad_maximum_fusion), calls=%async_computation | async-start | bytes 2097152 | tf_op jit(solution)/shard_map/all_to_all | solution.py:274
  (17 other events, 208.4 us)
